TPU v7x, 128 devices: a whole 4x4x4 slice. The times are simulated.
128 devices in a mesh: row: 8 (over x, core), col: 16 (over z, y).
Axes of the slice: x: 4, y: 4, z: 4, core: 2. Of those that a mesh axis runs over, the one named last changes fastest.
Arguments:
- sdf_grids: bfloat16 [65536, 4096], P(('row', 'col')), may hold values from -6 to 6
- grain_poses: float32 [12, 65536], P(None, ('row', 'col')), may hold values from -4 to 4
- surface_nodes: float32 [65536, 768], P(('row', 'col')), may hold values from -5 to 5
- send_list: int32 [8, 16, 8, 32], P('row', 'col'), may hold values from 0 to 511, as said below
- pair_first: int32 [16384], P(('row', 'col')), may hold values from 0 to 511
- pair_sdf: int32 [16384], P(('row', 'col')), may hold values from 0 to 767, as said below
- pair_pose: int32 [16384], P(('row', 'col')), may hold values from 0 to 4607, as said below
- pair_live: int32 [16384], P(('row', 'col')), may hold values from 0 to 1, as said below
- knot_cells: int32 [16384, 768], P(('row', 'col')), may hold values from 1 to 13
- offsets: float32 [16384, 768], P(('row', 'col')), may hold values from 0 to 1
Outputs:
- grain_loads: float32 [6, 65536], P(None, ('row', 'col'))
Inputs may be any that keep to these rules, and one draw needn't show every extreme that they name: `send_list`: the 8 lists of one device name distinct own grains each; list d is meant for the neighbour at offset d of the direction order; the neighbour's pairs name only slots of list d below a count from 8 to 32; on every device one of its 8 lists has count 32. `pair_sdf`: below 512: an own grain other than the first grain. From 512 on: ghost block d and slot s of an existing neighbour. `pair_pose`: names the pose of the same grain as pair_sdf: an own grain in the centre block, or the neighbour's listed grain. `pair_live`: on each device the live slots come first; their number is 128 divided by 1, 2 or 4, and some device has all slots live.
All inputs are finite; a program needn't handle non-finite values.
Results may differ from a plain program's by a relative error of at most 0.0057.
Values may be sent and summed in bfloat16 or wider, within the bound.
No kernel may reach another device: no remote copies, remote signals or barrier semaphores. Data moves between devices by JAX's collectives and lax.ppermute only.
A program may use at most 64 MiB of HBM per device.

v0:
```python
import jax
import jax.numpy as jnp
from jax import lax
from jax.sharding import PartitionSpec as P

GRID = 16


DIRECTIONS = ((-1, -1), (-1, 0), (-1, 1), (0, -1), (0, 1), (1, -1), (1, 0), (1, 1))
STIFFNESS = 0.25
pair_block = 32


def with_halo(block, sides, width):
    for axis, dim in sides:
        count = lax.axis_size(axis)
        forward = [(i, i + 1) for i in range(count - 1)]
        backward = [(target, source) for source, target in forward]
        low = lax.ppermute(
            lax.slice_in_dim(block, block.shape[dim] - width, None, axis=dim), axis, forward
        )
        high = lax.ppermute(lax.slice_in_dim(block, 0, width, axis=dim), axis, backward)
        block = jnp.concatenate([low, block, high], axis=dim)
    return block


def passed_along(block, axis, distance):
    devices = range(lax.axis_size(axis))
    route = [(i - distance, i) for i in devices if i - distance in devices]
    return lax.ppermute(block, axis, route)


def spline_tables(knot_cell, fraction):
    complement = 1.0 - fraction
    squared = fraction * fraction
    cubed = squared * fraction
    weights = (
        complement * complement * complement / 6.0,
        (3.0 * cubed - 6.0 * squared + 4.0) / 6.0,
        (-3.0 * cubed + 3.0 * squared + 3.0 * fraction + 1.0) / 6.0,
        cubed / 6.0,
    )
    slopes = (
        -0.5 * complement * complement,
        0.5 * (3.0 * squared - 4.0 * fraction),
        0.5 * (-3.0 * squared + 2.0 * fraction + 1.0),
        0.5 * squared,
    )
    cell_ids = jnp.arange(GRID, dtype=jnp.int32)[:, None]
    shape = knot_cell.shape[:2] + (GRID,) + knot_cell.shape[2:]
    basis_rows = jnp.zeros(shape, jnp.float32)
    slope_rows = jnp.zeros(shape, jnp.float32)
    for position in range(4):
        matches = cell_ids == (knot_cell + (position - 1))[:, :, None, :]
        basis_rows = basis_rows + jnp.where(
            matches, weights[position][:, :, None, :], jnp.float32(0.0)
        )
        slope_rows = slope_rows + jnp.where(
            matches, slopes[position][:, :, None, :], jnp.float32(0.0)
        )
    return (basis_rows, slope_rows)


def pair_terms(grid_rows, knot_cell, fraction, pose_first, pose_second, node_body):
    highest = lax.Precision.HIGHEST
    batch_size = grid_rows.shape[0]
    node_count = knot_cell.shape[2]
    basis_rows, slope_rows = spline_tables(knot_cell, fraction)
    x_basis = basis_rows[:, 0].astype(jnp.bfloat16)
    x_slope = slope_rows[:, 0].astype(jnp.bfloat16)
    grid_cube = grid_rows.reshape(batch_size, GRID, GRID * GRID)
    partial_plain = jnp.einsum(
        "pam,pan->pmn", grid_cube, x_basis, preferred_element_type=jnp.float32
    ).reshape(batch_size, GRID, GRID, node_count)
    partial_slope = jnp.einsum(
        "pam,pan->pmn", grid_cube, x_slope, preferred_element_type=jnp.float32
    ).reshape(batch_size, GRID, GRID, node_count)
    basis_y = basis_rows[:, 1]
    slope_y = slope_rows[:, 1]
    section_plain = jnp.einsum("pbcn,pbn->pcn", partial_plain, basis_y, precision=highest)
    section_xslope = jnp.einsum("pbcn,pbn->pcn", partial_slope, basis_y, precision=highest)
    section_yslope = jnp.einsum("pbcn,pbn->pcn", partial_plain, slope_y, precision=highest)
    basis_z = basis_rows[:, 2]
    slope_z = slope_rows[:, 2]
    distance = jnp.einsum("pcn,pcn->pn", section_plain, basis_z, precision=highest)
    gradient = jnp.stack(
        [
            jnp.einsum("pcn,pcn->pn", section_xslope, basis_z, precision=highest),
            jnp.einsum("pcn,pcn->pn", section_yslope, basis_z, precision=highest),
            jnp.einsum("pcn,pcn->pn", section_plain, slope_z, precision=highest),
        ],
        axis=1,
    )
    penetration = STIFFNESS * jax.nn.relu(-distance)
    rotation_second = pose_second[:, 3:].reshape(batch_size, 3, 3)
    rotation_first = pose_first[:, 3:].reshape(batch_size, 3, 3)
    normal = jnp.einsum("prc,pcn->prn", rotation_second, gradient, precision=highest)
    node_force = penetration[:, None, :] * normal
    lever_arm = jnp.einsum("prc,pcn->prn", rotation_first, node_body, precision=highest)
    net_force = jnp.sum(node_force, axis=2)
    moment = jnp.sum(jnp.cross(lever_arm, node_force, axis=1), axis=2)
    separation = pose_first[:, :3] - pose_second[:, :3]
    moment_other = -(jnp.cross(separation, net_force, axis=1) + moment)
    return (
        jnp.concatenate([net_force, moment], axis=1),
        jnp.concatenate([-net_force, moment_other], axis=1),
    )


def pair_loads(
    grid_table,
    pose_table,
    grain_poses,
    surface_nodes,
    pair_first,
    pair_sdf,
    pair_pose,
    pair_live,
    knot_cells,
    offsets,
):
    pair_count = pair_first.shape[0]
    node_count = knot_cells.shape[1] // 3
    block_size = min(pair_block, pair_count)
    grid_rows = jnp.take(grid_table, pair_sdf, axis=0)
    pose_first = jnp.take(grain_poses, pair_first, axis=1).T
    pose_second = jnp.take(pose_table, pair_pose, axis=1).T
    node_body = jnp.take(surface_nodes, pair_first, axis=0).reshape(pair_count, 3, node_count)
    knot_cell = knot_cells.reshape(pair_count, 3, node_count)
    fraction = offsets.reshape(pair_count, 3, node_count)
    pieces = (grid_rows, knot_cell, fraction, pose_first, pose_second, node_body)
    blocked = tuple(
        (item.reshape((pair_count // block_size, block_size) + item.shape[1:]) for item in pieces)
    )
    on_first, on_second = lax.map(lambda group: pair_terms(*group), blocked)
    alive_mask = pair_live.astype(jnp.float32)[:, None]
    on_first = on_first.reshape(pair_count, 6) * alive_mask
    on_second = on_second.reshape(pair_count, 6) * alive_mask
    return jax.ops.segment_sum(
        jnp.concatenate([on_first, on_second], axis=0),
        jnp.concatenate([pair_first, pair_sdf], axis=0),
        num_segments=grid_table.shape[0],
    )


def sectioned_routes(blocks, move_row, move_col):
    arrived = {}
    for col_step in (-1, 1):
        chosen = [direction for direction in range(8) if DIRECTIONS[direction][1] == col_step]
        carried = move_col(jnp.stack([blocks[7 - direction] for direction in chosen]), -col_step)
        for position, direction in enumerate(chosen):
            arrived[direction] = carried[position]
    for row_step in (-1, 1):
        chosen = [direction for direction in range(8) if DIRECTIONS[direction][0] == row_step]
        stacked = jnp.stack(
            [
                arrived[direction] if DIRECTIONS[direction][1] != 0 else blocks[7 - direction]
                for direction in chosen
            ]
        )
        carried = move_row(stacked, -row_step)
        for position, direction in enumerate(chosen):
            arrived[direction] = carried[position]
    return jnp.stack([arrived[direction] for direction in range(8)])


def local(
    sdf_grids,
    grain_poses,
    surface_nodes,
    send_list,
    pair_first,
    pair_sdf,
    pair_pose,
    pair_live,
    knot_cells,
    offsets,
):
    grains = sdf_grids.shape[0]
    capacity = send_list.shape[3]
    listed = send_list.reshape(8, capacity)
    outgoing = jnp.take(sdf_grids, listed.reshape(-1), axis=0).reshape(
        8, capacity, sdf_grids.shape[1]
    )
    pose_table = with_halo(grain_poses.reshape(12, 1, 1, grains), (("row", 1), ("col", 2)), 1)
    pose_table = pose_table.reshape(12, 9 * grains)
    received = sectioned_routes(
        outgoing,
        lambda payload, offset: passed_along(payload, "row", offset),
        lambda payload, offset: passed_along(payload, "col", offset),
    )
    grid_table = jnp.concatenate(
        [sdf_grids, received.reshape(8 * capacity, sdf_grids.shape[1])], axis=0
    )
    slot_sums = pair_loads(
        grid_table,
        pose_table,
        grain_poses,
        surface_nodes,
        pair_first,
        pair_sdf,
        pair_pose,
        pair_live,
        knot_cells,
        offsets,
    )
    owned_sum = slot_sums[:grains]
    reaction = slot_sums[grains:].reshape(8, capacity, 6)
    returned = sectioned_routes(
        reaction,
        lambda payload, offset: passed_along(payload, "row", offset),
        lambda payload, offset: passed_along(payload, "col", offset),
    )
    owned_sum = owned_sum + jax.ops.segment_sum(
        returned.reshape(8 * capacity, 6), listed.reshape(-1), num_segments=grains
    )
    return owned_sum.T


def solution(mesh):
    in_specs = (
        P(("row", "col"), None),
        P(None, ("row", "col")),
        P(("row", "col"), None),
        P("row", "col", None, None),
        P(("row", "col")),
        P(("row", "col")),
        P(("row", "col")),
        P(("row", "col")),
        P(("row", "col"), None),
        P(("row", "col"), None),
    )
    out_specs = P(None, ("row", "col"))
    return jax.shard_map(local, mesh=mesh, in_specs=in_specs, out_specs=out_specs, check_vma=False)
```

profile of v0, /device:TPU:25, one launch (start us, length us, event | category | flops | bytes accessed | tf_op | source)
XLA Modules:
  0.0 167.7 jit_solution(8584697781385178476)
XLA Ops:
  0.0 3.8 %collective-permute-start.4 = (f32[12,1,1,512]{3,0,2,1:T(8,128)}, f32[12,1,1,512]{3,0,2,1:T(8,128)}, u32[]{:S(2)}, u32[]{:S(2)}) collective-permute-start(f32[12,1,1,512]{3,0,2,1:T(8,128)} %bitcast.243), channel_id=1, source_target_pairs={{0,16},{16,32},{32,48},{48,64},{64,80},{80,96},{96,112},{1,17},{17... | collective-permute-start | bytes 73736 | tf_op jit(solution)/shard_map/ppermute | solution.py:19
  3.8 1.9 %collective-permute-start.5 = (f32[12,1,1,512]{3,0,2,1:T(8,128)}, f32[12,1,1,512]{3,0,2,1:T(8,128)}, u32[]{:S(2)}, u32[]{:S(2)}) collective-permute-start(f32[12,1,1,512]{3,0,2,1:T(8,128)} %bitcast.244), channel_id=1, source_target_pairs={{16,0},{32,16},{48,32},{64,48},{80,64},{96,80},{112,96},{17,1},{33... | collective-permute-start | bytes 73736 | tf_op jit(solution)/shard_map/ppermute | solution.py:22
  7.3 8.0 %gather_fusion = bf16[256,4096]{1,0:T(8,128)(2,1)} fusion(bf16[512,4096]{1,0:T(8,128)(2,1)} %param.12, s32[1024]{0:T(1024)S(1)} %pad_clamp_fusion.3), kind=kCustom, calls=%fused_computation | custom fusion | bytes 4195328 | tf_op jit(solution)/shard_map/jit(_take)/gather | solution.py:182
  15.3 1.8 %broadcast_select_fusion = bf16[256,4096]{1,0:T(8,128)(2,1)S(1)} fusion(bf16[256,4096]{1,0:T(8,128)(2,1)} %gather_fusion, pred[256]{0:T(512)(128)(4,1)S(1)} %compare_and_fusion.2), kind=kLoop, calls=%fused_computation.89 | loop fusion | flops 1048576 | bytes 4194560 | tf_op jit(solution)/shard_map/jit(_take)/select_n | solution.py:182
  19.0 3.2 %collective-permute-start = (bf16[3,32,4096]{2,1,0:T(8,128)(2,1)}, bf16[3,32,4096]{2,1,0:T(8,128)(2,1)}, u32[]{:S(2)}, u32[]{:S(2)}) collective-permute-start(bf16[3,32,4096]{2,1,0:T(8,128)(2,1)} %pad_maximum_fusion.2), channel_id=1, source_target_pairs={{0,1},{1,2},{2,3},{3,4},{4,5},{5,6},{6,7},{7,8},{8,9},{9,10},{10,1... | collective-permute-start | bytes 2359304 | tf_op jit(solution)/shard_map/ppermute | solution.py:30
  23.1 2.1 %collective-permute-start.1 = (bf16[3,32,4096]{2,1,0:T(8,128)(2,1)}, bf16[3,32,4096]{2,1,0:T(8,128)(2,1)}, u32[]{:S(2)}, u32[]{:S(2)}) collective-permute-start(bf16[3,32,4096]{2,1,0:T(8,128)(2,1)} %pad_maximum_fusion.3), channel_id=1, source_target_pairs={{1,0},{2,1},{3,2},{4,3},{5,4},{6,5},{7,6},{8,7},{9,8},{10,9},{11,1... | collective-permute-start | bytes 2359304 | tf_op jit(solution)/shard_map/ppermute | solution.py:30
  29.7 10.2 %collective-permute-done = bf16[3,32,4096]{2,1,0:T(8,128)(2,1)} collective-permute-done((bf16[3,32,4096]{2,1,0:T(8,128)(2,1)}, bf16[3,32,4096]{2,1,0:T(8,128)(2,1)}, u32[]{:S(2)}, u32[]{:S(2)}) %collective-permute-start) | collective-permute-done | bytes 786464 | tf_op jit(solution)/shard_map/ppermute | solution.py:30
  41.0 5.1 %collective-permute-done.1 = bf16[3,32,4096]{2,1,0:T(8,128)(2,1)} collective-permute-done((bf16[3,32,4096]{2,1,0:T(8,128)(2,1)}, bf16[3,32,4096]{2,1,0:T(8,128)(2,1)}, u32[]{:S(2)}, u32[]{:S(2)}) %collective-permute-start.1) | collective-permute-done | bytes 786464 | tf_op jit(solution)/shard_map/ppermute | solution.py:30
  48.3 4.3 %collective-permute-start.2 = (bf16[3,32,4096]{2,1,0:T(8,128)(2,1)}, bf16[3,32,4096]{2,1,0:T(8,128)(2,1)}, u32[]{:S(2)}, u32[]{:S(2)}) collective-permute-start(bf16[3,32,4096]{2,1,0:T(8,128)(2,1)} %pad_maximum_fusion.4), channel_id=1, source_target_pairs={{0,16},{16,32},{32,48},{48,64},{64,80},{80,96},{96,112},{1,17},{17... | collective-permute-start | bytes 2359304 | tf_op jit(solution)/shard_map/ppermute | solution.py:30
  53.6 1.9 %collective-permute-start.3 = (bf16[3,32,4096]{2,1,0:T(8,128)(2,1)}, bf16[3,32,4096]{2,1,0:T(8,128)(2,1)}, u32[]{:S(2)}, u32[]{:S(2)}) collective-permute-start(bf16[3,32,4096]{2,1,0:T(8,128)(2,1)} %pad_maximum_fusion.5), channel_id=1, source_target_pairs={{16,0},{32,16},{48,32},{64,48},{80,64},{96,80},{112,96},{17,1},{33... | collective-permute-start | bytes 2359304 | tf_op jit(solution)/shard_map/ppermute | solution.py:30
  61.0 1.9 %collective-permute-start.6 = (f32[12,3,1,512]{3,0,2,1:T(8,128)S(1)}, f32[12,3,1,512]{3,0,2,1:T(8,128)S(1)}, u32[]{:S(2)}, u32[]{:S(2)}) collective-permute-start(f32[12,3,1,512]{3,0,2,1:T(8,128)S(1)} %pad_maximum_fusion.7), channel_id=1, source_target_pairs={{0,1},{1,2},{2,3},{3,4},{4,5},{5,6},{6,7},{7,8},{8,9},{9,10},{10,1... | collective-permute-start | bytes 221192 | tf_op jit(solution)/shard_map/ppermute | solution.py:19
  63.0 3.4 %collective-permute-start.7 = (f32[12,3,1,512]{3,0,2,1:T(8,128)S(1)}, f32[12,3,1,512]{3,0,2,1:T(8,128)S(1)}, u32[]{:S(2)}, u32[]{:S(2)}) collective-permute-start(f32[12,3,1,512]{3,0,2,1:T(8,128)S(1)} %pad_maximum_fusion.7), channel_id=1, source_target_pairs={{1,0},{2,1},{3,2},{4,3},{5,4},{6,5},{7,6},{8,7},{9,8},{10,9},{11,1... | collective-permute-start | bytes 221192 | tf_op jit(solution)/shard_map/ppermute | solution.py:22
  66.9 3.5 %collective-permute-done.7 = f32[12,3,1,512]{3,0,2,1:T(8,128)S(1)} collective-permute-done((f32[12,3,1,512]{3,0,2,1:T(8,128)S(1)}, f32[12,3,1,512]{3,0,2,1:T(8,128)S(1)}, u32[]{:S(2)}, u32[]{:S(2)}) %collective-permute-start.7) | collective-permute-done | bytes 73760 | tf_op jit(solution)/shard_map/ppermute | solution.py:22
  71.2 2.1 %copy.224 = f32[12,3,3,512]{0,3,2,1:T(8,128)} copy(f32[12,3,3,512]{3,0,2,1:T(8,128)S(1)} %pad_maximum_fusion.6) | data formatting | bytes 442368 | tf_op jit(solution)/shard_map/concatenate | solution.py:23
  73.4 2.3 %gather_fusion.2 = f32[128,12]{1,0:T(8,128)S(1)} fusion(f32[12,4608]{0,1:T(8,128)} %bitcast.239, s32[1024]{0:T(1024)S(1)} %pad_clamp_fusion.1), kind=kCustom, calls=%fused_computation.2 | custom fusion | bytes 12800 | tf_op jit(solution)/shard_map/jit(_take)/gather | solution.py:127
  76.4 1.8 %pad_maximum_fusion.1 = bf16[8,32,4096]{2,1,0:T(8,128)(2,1)S(1)} fusion(bf16[3,32,4096]{2,1,0:T(8,128)(2,1)} %collective-permute-done.3, bf16[1,32,4096]{2,1,0:T(8,128)(2,1)S(1)} %get-tuple-element.209, bf16[1,32,4096]{2,1,0:T(8,128)(2,1)S(1)} %get-tuple-element.206, bf16[3,32,4096]{2,1,0:T(8,128)(2,1)} %collective-permute-done.2), kind=kLoop, calls=%fused_computation.88 | loop fusion | flops 3145728 | bytes 4194304 | tf_op jit(solution)/shard_map/stack | solution.py:164
  79.1 3.4 %pad_maximum_fusion = bf16[768,4096]{1,0:T(8,128)(2,1)} fusion(bf16[256,4096]{1,0:T(8,128)(2,1)S(1)} %bitcast.237, bf16[512,4096]{1,0:T(8,128)(2,1)S(1)} %copy-done.1), kind=kLoop, calls=%fused_computation.87 | loop fusion | flops 12582912 | bytes 12582912 | tf_op jit(solution)/shard_map/concatenate | solution.py:192
  82.5 6.8 %gather_fusion.1 = bf16[128,4096]{1,0:T(8,128)(2,1)} fusion(bf16[768,4096]{1,0:T(8,128)(2,1)} %pad_maximum_fusion, s32[1024]{0:T(1024)S(1)} %pad_clamp_fusion.2), kind=kCustom, calls=%fused_computation.1 | custom fusion | bytes 2097664 | tf_op jit(solution)/shard_map/jit(_take)/gather | solution.py:125
  89.3 1.4 broadcast_select_fusion.1
  90.7 52.0 %while.12 = (s32[]{:T(128)}, f32[4,32,6]{1,0,2:T(4,128)S(1)}, f32[4,32,6]{1,0,2:T(4,128)S(1)}, s32[4,32,3,256]{3,1,2,0:T(8,128)}, f32[4,32,3,256]{3,1,2,0:T(8,12...) while((s32[]{:T(128)}, f32[4,32,6]{1,0,2:T(4,128)S(1)}, ...), condition=%wide.region_3.4_spmd, body=%wide.region_0.3_spmd.sunk | while | flops 157352992 | bytes 50134664 | solution.py:135
  96.9 3.4 %multiply_reduce_fusion.8 = (f32[32,256,16]{1,2,0:T(8,128)S(1)}, f32[32,256,16]{1,2,0:T(8,128)S(1)}, f32[32,256,16]{1,2,0:T(8,128)S(1)}) fusion(f32[32,256,16,16]{1,3,2,0:T(8,128)S(1)} %bitcast.232, f32[32,256,16]{1,2,0:T(8,128)S(1)} %get-tuple-element.329, f32[32,256,16]{1,2,0:T(8,128)S(1)} %get-tuple-element.330, f32[32,256,16,16]{1,3,2,0:T(8,128)S(1)} %bitcast.231), kind=kLoop, calls=%fused_computation.7.clone.1 | loop fusion | flops 12189696 | bytes 19398656 | tf_op jit(solution)/shard_map/while/body/eval_jaxpr/pbcn,pbn->pcn/dot_general | solution.py:82
  109.9 3.4 %multiply_reduce_fusion.8 = (f32[32,256,16]{1,2,0:T(8,128)S(1)}, f32[32,256,16]{1,2,0:T(8,128)S(1)}, f32[32,256,16]{1,2,0:T(8,128)S(1)}) fusion(f32[32,256,16,16]{1,3,2,0:T(8,128)S(1)} %bitcast.232, f32[32,256,16]{1,2,0:T(8,128)S(1)} %get-tuple-element.329, f32[32,256,16]{1,2,0:T(8,128)S(1)} %get-tuple-element.330, f32[32,256,16,16]{1,3,2,0:T(8,128)S(1)} %bitcast.231), kind=kLoop, calls=%fused_computation.7.clone.1 | loop fusion | flops 12189696 | bytes 19398656 | tf_op jit(solution)/shard_map/while/body/eval_jaxpr/pbcn,pbn->pcn/dot_general | solution.py:82
  122.9 3.4 %multiply_reduce_fusion.8 = (f32[32,256,16]{1,2,0:T(8,128)S(1)}, f32[32,256,16]{1,2,0:T(8,128)S(1)}, f32[32,256,16]{1,2,0:T(8,128)S(1)}) fusion(f32[32,256,16,16]{1,3,2,0:T(8,128)S(1)} %bitcast.232, f32[32,256,16]{1,2,0:T(8,128)S(1)} %get-tuple-element.329, f32[32,256,16]{1,2,0:T(8,128)S(1)} %get-tuple-element.330, f32[32,256,16,16]{1,3,2,0:T(8,128)S(1)} %bitcast.231), kind=kLoop, calls=%fused_computation.7.clone.1 | loop fusion | flops 12189696 | bytes 19398656 | tf_op jit(solution)/shard_map/while/body/eval_jaxpr/pbcn,pbn->pcn/dot_general | solution.py:82
  135.8 3.4 %multiply_reduce_fusion.8 = (f32[32,256,16]{1,2,0:T(8,128)S(1)}, f32[32,256,16]{1,2,0:T(8,128)S(1)}, f32[32,256,16]{1,2,0:T(8,128)S(1)}) fusion(f32[32,256,16,16]{1,3,2,0:T(8,128)S(1)} %bitcast.232, f32[32,256,16]{1,2,0:T(8,128)S(1)} %get-tuple-element.329, f32[32,256,16]{1,2,0:T(8,128)S(1)} %get-tuple-element.330, f32[32,256,16,16]{1,3,2,0:T(8,128)S(1)} %bitcast.231), kind=kLoop, calls=%fused_computation.7.clone.1 | loop fusion | flops 12189696 | bytes 19398656 | tf_op jit(solution)/shard_map/while/body/eval_jaxpr/pbcn,pbn->pcn/dot_general | solution.py:82
  143.1 1.7 scatter_custom_fusion
  145.0 1.9 %collective-permute-start.8 = (f32[3,32,6]{1,2,0:T(8,128)S(1)}, f32[3,32,6]{1,2,0:T(8,128)S(1)}, u32[]{:S(2)}, u32[]{:S(2)}) collective-permute-start(f32[3,32,6]{1,2,0:T(8,128)S(1)} %pad_maximum_fusion.9), channel_id=1, source_target_pairs={{0,1},{1,2},{2,3},{3,4},{4,5},{5,6},{6,7},{7,8},{8,9},{9,10},{10,1... | collective-permute-start | bytes 6920 | tf_op jit(solution)/shard_map/ppermute | solution.py:30
  147.2 3.4 %collective-permute-start.9 = (f32[3,32,6]{1,2,0:T(8,128)S(1)}, f32[3,32,6]{1,2,0:T(8,128)S(1)}, u32[]{:S(2)}, u32[]{:S(2)}) collective-permute-start(f32[3,32,6]{1,2,0:T(8,128)S(1)} %pad_maximum_fusion.10), channel_id=1, source_target_pairs={{1,0},{2,1},{3,2},{4,3},{5,4},{6,5},{7,6},{8,7},{9,8},{10,9},{11,1... | collective-permute-start | bytes 6920 | tf_op jit(solution)/shard_map/ppermute | solution.py:30
  150.7 3.4 %collective-permute-done.9 = f32[3,32,6]{1,2,0:T(8,128)S(1)} collective-permute-done((f32[3,32,6]{1,2,0:T(8,128)S(1)}, f32[3,32,6]{1,2,0:T(8,128)S(1)}, u32[]{:S(2)}, u32[]{:S(2)}) %collective-permute-start.9) | collective-permute-done | bytes 2336 | tf_op jit(solution)/shard_map/ppermute | solution.py:30
  154.2 5.5 %collective-permute-start.10 = (f32[3,32,6]{1,2,0:T(8,128)S(1)}, f32[3,32,6]{1,2,0:T(8,128)S(1)}, u32[]{:S(2)}, u32[]{:S(2)}) collective-permute-start(f32[3,32,6]{1,2,0:T(8,128)S(1)} %pad_maximum_fusion.11), channel_id=1, source_target_pairs={{0,16},{16,32},{32,48},{48,64},{64,80},{80,96},{96,112},{1,17},{17... | collective-permute-start | bytes 6920 | tf_op jit(solution)/shard_map/ppermute | solution.py:30
  159.7 1.9 %collective-permute-start.11 = (f32[3,32,6]{1,2,0:T(8,128)S(1)}, f32[3,32,6]{1,2,0:T(8,128)S(1)}, u32[]{:S(2)}, u32[]{:S(2)}) collective-permute-start(f32[3,32,6]{1,2,0:T(8,128)S(1)} %pad_maximum_fusion.12), channel_id=1, source_target_pairs={{16,0},{32,16},{48,32},{64,48},{80,64},{96,80},{112,96},{17,1},{33... | collective-permute-start | bytes 6920 | tf_op jit(solution)/shard_map/ppermute | solution.py:30
  161.7 3.0 %collective-permute-done.11 = f32[3,32,6]{1,2,0:T(8,128)S(1)} collective-permute-done((f32[3,32,6]{1,2,0:T(8,128)S(1)}, f32[3,32,6]{1,2,0:T(8,128)S(1)}, u32[]{:S(2)}, u32[]{:S(2)}) %collective-permute-start.11) | collective-permute-done | bytes 2336 | tf_op jit(solution)/shard_map/ppermute | solution.py:30
  164.9 2.0 %scatter_fusion = f32[512,6]{1,0:T(8,128)S(1)} fusion(f32[512,6]{1,0:T(8,128)S(1)} %slice.331, s32[256]{0:T(256)S(1)} %copy-done.7, f32[256,6]{1,0:T(8,128)S(1)} %bitcast.241), kind=kCustom, calls=%fused_computation.6 | custom fusion | flops 1536 | bytes 19456 | tf_op jit(solution)/shard_map/scatter-add | solution.py:214
  (251 shorter events, 61.0 us)
Async XLA Ops:
  0.0 27.0 %copy-start = (f32[512,768]{1,0:T(8,128)S(1)}, f32[512,768]{1,0:T(8,128)}, u32[]{:S(2)}) copy-start(f32[512,768]{1,0:T(8,128)} %param.14) | copy-start | bytes 4718596
  0.0 60.3 %collective-permute-start.4 = (f32[12,1,1,512]{3,0,2,1:T(8,128)}, f32[12,1,1,512]{3,0,2,1:T(8,128)}, u32[]{:S(2)}, u32[]{:S(2)}) collective-permute-start(f32[12,1,1,512]{3,0,2,1:T(8,128)} %bitcast.243), channel_id=1, source_target_pairs={{0,16},{16,32},{32,48},{48,64},{64,80},{80,96},{96,112},{1,17},{17... | collective-permute-start | bytes 73736 | tf_op jit(solution)/shard_map/ppermute | solution.py:19
  3.8 56.4 %collective-permute-start.5 = (f32[12,1,1,512]{3,0,2,1:T(8,128)}, f32[12,1,1,512]{3,0,2,1:T(8,128)}, u32[]{:S(2)}, u32[]{:S(2)}) collective-permute-start(f32[12,1,1,512]{3,0,2,1:T(8,128)} %bitcast.244), channel_id=1, source_target_pairs={{16,0},{32,16},{48,32},{64,48},{80,64},{96,80},{112,96},{17,1},{33... | collective-permute-start | bytes 73736 | tf_op jit(solution)/shard_map/ppermute | solution.py:22
  6.5 0.8 copy-start.6
  18.0 7.2 %copy-start.11 = (s32[128]{0:T(128)S(1)}, s32[128]{0:T(128)}, u32[]{:S(2)}) copy-start(s32[128]{0:T(128)} %param.17) | copy-start | bytes 1540
  18.0 8.3 %copy-start.13 = (s32[128]{0:T(128)S(1)}, s32[128]{0:T(128)}, u32[]{:S(2)}) copy-start(s32[128]{0:T(128)} %param.16) | copy-start | bytes 1540
  18.0 8.3 %copy-start.3 = (f32[12,512]{1,0:T(8,128)S(1)}, f32[12,512]{1,0:T(8,128)}, u32[]{:S(2)}) copy-start(f32[12,512]{1,0:T(8,128)} %param.13) | copy-start | bytes 73732
  18.0 8.4 %copy-start.15 = (s32[128]{0:T(128)S(1)}, s32[128]{0:T(128)}, u32[]{:S(2)}) copy-start(s32[128]{0:T(128)} %param.18) | copy-start | bytes 1540
  19.0 20.9 %collective-permute-start = (bf16[3,32,4096]{2,1,0:T(8,128)(2,1)}, bf16[3,32,4096]{2,1,0:T(8,128)(2,1)}, u32[]{:S(2)}, u32[]{:S(2)}) collective-permute-start(bf16[3,32,4096]{2,1,0:T(8,128)(2,1)} %pad_maximum_fusion.2), channel_id=1, source_target_pairs={{0,1},{1,2},{2,3},{3,4},{4,5},{5,6},{6,7},{7,8},{8,9},{9,10},{10,1... | collective-permute-start | bytes 2359304 | tf_op jit(solution)/shard_map/ppermute | solution.py:30
  23.1 23.0 %collective-permute-start.1 = (bf16[3,32,4096]{2,1,0:T(8,128)(2,1)}, bf16[3,32,4096]{2,1,0:T(8,128)(2,1)}, u32[]{:S(2)}, u32[]{:S(2)}) collective-permute-start(bf16[3,32,4096]{2,1,0:T(8,128)(2,1)} %pad_maximum_fusion.3), channel_id=1, source_target_pairs={{1,0},{2,1},{3,2},{4,3},{5,4},{6,5},{7,6},{8,7},{9,8},{10,9},{11,1... | collective-permute-start | bytes 2359304 | tf_op jit(solution)/shard_map/ppermute | solution.py:30
  29.7 17.6 %copy-start.2 = (bf16[1,32,4096]{2,1,0:T(8,128)(2,1)S(1)}, bf16[1,32,4096]{2,1,0:T(8,128)(2,1)}, u32[]{:S(2)}) copy-start(bf16[1,32,4096]{2,1,0:T(8,128)(2,1)} %get-tuple-element.196) | copy-start | bytes 786436
  47.3 8.2 %copy-start.9 = (s32[128]{0:T(128)S(1)}, s32[128]{0:T(128)}, u32[]{:S(2)}) copy-start(s32[128]{0:T(128)} %compare_select_fusion.4) | copy-start | bytes 1540
  47.3 8.2 %copy-start.10 = (s32[128]{0:T(128)S(1)}, s32[128]{0:T(128)}, u32[]{:S(2)}) copy-start(s32[128]{0:T(128)} %compare_select_fusion.3) | copy-start | bytes 1540
  47.3 8.2 %copy-start.17 = (pred[128]{0:T(512)(128)(4,1)S(1)}, pred[128]{0:T(512)(128)(4,1)}, u32[]{:S(2)}) copy-start(pred[128]{0:T(512)(128)(4,1)} %compare_and_fusion.3) | copy-start | bytes 388
  48.3 28.1 %collective-permute-start.2 = (bf16[3,32,4096]{2,1,0:T(8,128)(2,1)}, bf16[3,32,4096]{2,1,0:T(8,128)(2,1)}, u32[]{:S(2)}, u32[]{:S(2)}) collective-permute-start(bf16[3,32,4096]{2,1,0:T(8,128)(2,1)} %pad_maximum_fusion.4), channel_id=1, source_target_pairs={{0,16},{16,32},{32,48},{48,64},{64,80},{80,96},{96,112},{1,17},{17... | collective-permute-start | bytes 2359304 | tf_op jit(solution)/shard_map/ppermute | solution.py:30
  53.6 22.8 %collective-permute-start.3 = (bf16[3,32,4096]{2,1,0:T(8,128)(2,1)}, bf16[3,32,4096]{2,1,0:T(8,128)(2,1)}, u32[]{:S(2)}, u32[]{:S(2)}) collective-permute-start(bf16[3,32,4096]{2,1,0:T(8,128)(2,1)} %pad_maximum_fusion.5), channel_id=1, source_target_pairs={{16,0},{32,16},{48,32},{64,48},{80,64},{96,80},{112,96},{17,1},{33... | collective-permute-start | bytes 2359304 | tf_op jit(solution)/shard_map/ppermute | solution.py:30
  56.9 2.9 %copy-start.16 = (s32[128]{0:T(128)S(1)}, s32[128]{0:T(128)}, u32[]{:S(2)}) copy-start(s32[128]{0:T(128)} %param.19) | copy-start | bytes 1540
  56.9 9.5 %copy-start.12 = (s32[128]{0:T(128)S(1)}, s32[128]{0:T(128)}, u32[]{:S(2)}) copy-start(s32[128]{0:T(128)} %param.17) | copy-start | bytes 1540
  56.9 9.5 %copy-start.14 = (s32[128]{0:T(128)S(1)}, s32[128]{0:T(128)}, u32[]{:S(2)}) copy-start(s32[128]{0:T(128)} %param.16) | copy-start | bytes 1540
  61.0 5.9 %collective-permute-start.6 = (f32[12,3,1,512]{3,0,2,1:T(8,128)S(1)}, f32[12,3,1,512]{3,0,2,1:T(8,128)S(1)}, u32[]{:S(2)}, u32[]{:S(2)}) collective-permute-start(f32[12,3,1,512]{3,0,2,1:T(8,128)S(1)} %pad_maximum_fusion.7), channel_id=1, source_target_pairs={{0,1},{1,2},{2,3},{3,4},{4,5},{5,6},{6,7},{7,8},{8,9},{9,10},{10,1... | collective-permute-start | bytes 221192 | tf_op jit(solution)/shard_map/ppermute | solution.py:19
  63.0 7.5 %collective-permute-start.7 = (f32[12,3,1,512]{3,0,2,1:T(8,128)S(1)}, f32[12,3,1,512]{3,0,2,1:T(8,128)S(1)}, u32[]{:S(2)}, u32[]{:S(2)}) collective-permute-start(f32[12,3,1,512]{3,0,2,1:T(8,128)S(1)} %pad_maximum_fusion.7), channel_id=1, source_target_pairs={{1,0},{2,1},{3,2},{4,3},{5,4},{6,5},{7,6},{8,7},{9,8},{10,9},{11,1... | collective-permute-start | bytes 221192 | tf_op jit(solution)/shard_map/ppermute | solution.py:22
  76.4 2.7 %copy-start.1 = (bf16[512,4096]{1,0:T(8,128)(2,1)S(1)}, bf16[512,4096]{1,0:T(8,128)(2,1)}, u32[]{:S(2)}) copy-start(bf16[512,4096]{1,0:T(8,128)(2,1)} %param.12) | copy-start | bytes 12582916
  89.3 1.4 copy-start.4
  89.3 1.4 copy-start.5
  90.7 52.2 %copy-start.8 = (f32[128]{0:T(128)S(1)}, f32[128]{0:T(128)}, u32[]{:S(2)}) copy-start(f32[128]{0:T(128)} %convert_element_type.11) | copy-start | bytes 1540
  142.8 22.1 %copy-start.7 = (s32[256]{0:T(256)S(1)}, s32[256]{0:T(256)}, u32[]{:S(2)}) copy-start(s32[256]{0:T(256)} %copy-done.6) | copy-start | bytes 3076
  145.0 5.7 %collective-permute-start.8 = (f32[3,32,6]{1,2,0:T(8,128)S(1)}, f32[3,32,6]{1,2,0:T(8,128)S(1)}, u32[]{:S(2)}, u32[]{:S(2)}) collective-permute-start(f32[3,32,6]{1,2,0:T(8,128)S(1)} %pad_maximum_fusion.9), channel_id=1, source_target_pairs={{0,1},{1,2},{2,3},{3,4},{4,5},{5,6},{6,7},{7,8},{8,9},{9,10},{10,1... | collective-permute-start | bytes 6920 | tf_op jit(solution)/shard_map/ppermute | solution.py:30
  147.2 7.0 %collective-permute-start.9 = (f32[3,32,6]{1,2,0:T(8,128)S(1)}, f32[3,32,6]{1,2,0:T(8,128)S(1)}, u32[]{:S(2)}, u32[]{:S(2)}) collective-permute-start(f32[3,32,6]{1,2,0:T(8,128)S(1)} %pad_maximum_fusion.10), channel_id=1, source_target_pairs={{1,0},{2,1},{3,2},{4,3},{5,4},{6,5},{7,6},{8,7},{9,8},{10,9},{11,1... | collective-permute-start | bytes 6920 | tf_op jit(solution)/shard_map/ppermute | solution.py:30
  154.2 7.5 %collective-permute-start.10 = (f32[3,32,6]{1,2,0:T(8,128)S(1)}, f32[3,32,6]{1,2,0:T(8,128)S(1)}, u32[]{:S(2)}, u32[]{:S(2)}) collective-permute-start(f32[3,32,6]{1,2,0:T(8,128)S(1)} %pad_maximum_fusion.11), channel_id=1, source_target_pairs={{0,16},{16,32},{32,48},{48,64},{64,80},{80,96},{96,112},{1,17},{17... | collective-permute-start | bytes 6920 | tf_op jit(solution)/shard_map/ppermute | solution.py:30
  159.7 5.0 %collective-permute-start.11 = (f32[3,32,6]{1,2,0:T(8,128)S(1)}, f32[3,32,6]{1,2,0:T(8,128)S(1)}, u32[]{:S(2)}, u32[]{:S(2)}) collective-permute-start(f32[3,32,6]{1,2,0:T(8,128)S(1)} %pad_maximum_fusion.12), channel_id=1, source_target_pairs={{16,0},{32,16},{48,32},{64,48},{80,64},{96,80},{112,96},{17,1},{33... | collective-permute-start | bytes 6920 | tf_op jit(solution)/shard_map/ppermute | solution.py:30
where the time goes:
time: 169 us; the launch traced here: 168 us
  other arithmetic  53.1 us (31%)
  local copies, waits for them, and re-layouts  38.9 us (23%)
  starting transfers between devices  35.2 us (21%)
  waiting for transfers between devices  25.3 us (15%)
  matrix products  13.9 us (8%)
    ppermute x8, starting transfers between devices, passed_along(): return lax.ppermute(block, axis, route)  24.2 us
    ppermute x8, waiting for transfers between devices, passed_along(): return lax.ppermute(block, axis, route)  21.7 us
    dot_general x4, other arithmetic, pair_terms(): jnp.einsum('pbcn,pbn->pcn', partial_plain, slope_y, precision=highest)  13.4 us
    gather x1, local copies, waits for them, and re-layouts, local(): jnp.take(sdf_grids, listed.reshape(-1), axis=0)  7.96 us
    gather x1, local copies, waits for them, and re-layouts, pair_loads(): grid_rows = jnp.take(grid_table, pair_sdf, axis=0)  6.79 us
    ppermute x2, starting transfers between devices, with_halo(): lax.ppermute(lax.slice_in_dim(block, block.shape[dim] - width, None, axis...  5.72 us
    ppermute x2, starting transfers between devices, with_halo(): lax.ppermute(lax.slice_in_dim(block, 0, width, axis=dim), axis, backward)  5.29 us
    add x4, other arithmetic, spline_tables(): slope_rows + jnp.where(matches, slopes[position][:, :, None, :], jnp.floa...  5.19 us
  transfers between devices with their start and end apart: 12, of which 5 were waited for; matrix products, arithmetic and copies ran while one was open for 21% of the time, Pallas kernels for 0%

commit v1 on v0

v1 whole, which is shorter than its diff:
```python
import functools

import jax
import jax.numpy as jnp
from jax import lax
from jax.experimental import pallas as pl
from jax.experimental.pallas import tpu as pltpu
from jax.sharding import PartitionSpec as P

GRID = 16
STIFFNESS = 0.25
OPS = ("C", "D", "AC", "AD", "BC", "BD", "A", "B")
F32 = jnp.float32
BF16 = jnp.bfloat16
NN = (((1,), (0,)), ((), ()))
NT = (((1,), (1,)), ((), ()))


def steps_of(op):
    row = 1 if "A" in op else (-1 if "B" in op else 0)
    col = 1 if "C" in op else (-1 if "D" in op else 0)
    return row, col


def direction_of(row_step, col_step):
    cell = (row_step + 1) * 3 + col_step + 1
    return cell - (cell > 4).astype(jnp.int32)


def parity_signs():
    return 1 - 2 * (lax.axis_index("row") & 1), 1 - 2 * (lax.axis_index("col") & 1)


def split3(value):
    high = value.astype(BF16)
    rest = value - high.astype(F32)
    middle = rest.astype(BF16)
    low = (rest - middle.astype(F32)).astype(BF16)
    return high, middle, low


def dot(left, right, dims=NN):
    return lax.dot_general(left, right, dims, preferred_element_type=F32)


def listed_column(listed, signs, op):
    row_step, col_step = steps_of(op)
    direction = direction_of(row_step * signs[0], col_step * signs[1])
    row = listed[pl.ds(direction, 1), :].astype(F32)
    size = row.shape[1]
    eye = lax.broadcasted_iota(jnp.int32, (size, size), 0) == lax.broadcasted_iota(jnp.int32, (size, size), 1)
    return jnp.sum(jnp.where(eye, row, 0.0), axis=1, keepdims=True)


def one_hot_rows(column, width):
    lanes = lax.broadcasted_iota(jnp.int32, (column.shape[0], width), 1).astype(F32)
    return jnp.where(lanes == column, 1.0, 0.0).astype(BF16)


def pose_pieces(poses, pieces, padded):
    padded[...] = jnp.zeros_like(padded)
    padded[0:12, :] = poses[...]
    for index, piece in enumerate(split3(padded[...])):
        pieces[16 * index:16 * index + 16, :] = piece


def pack_kernel(listed, poses, grids, *refs):
    outs = refs[:8]
    table, hot, padded, pieces, sems = refs[8:]
    chunks = sems.shape[0]
    width = grids.shape[1] // chunks
    copies = []
    for index in range(chunks):
        part = pl.ds(index * width, width)
        copy = pltpu.make_async_copy(grids.at[:, part], table.at[:, part], sems.at[index])
        copy.start()
        copies.append(copy)
    signs = parity_signs()
    grains = grids.shape[0]
    for index, op in enumerate(OPS):
        hot[32 * index:32 * index + 32, :] = one_hot_rows(listed_column(listed, signs, op), grains)
    pieces[...] = jnp.zeros_like(pieces)
    pose_pieces(poses, pieces, padded)
    chosen = dot(hot[...], pieces[...], NT).astype(BF16)
    for index in range(8):
        outs[index][:, chunks * width:] = chosen[32 * index:32 * index + 32]
    for step in range(chunks):
        copies[step].wait()
        part = slice(step * width, step * width + width)
        rows = dot(hot[...], table[:, part]).astype(BF16)
        for index in range(8):
            outs[index][:, part] = rows[32 * index:32 * index + 32]


def pack(listed, poses, grids):
    grains, cells = grids.shape
    vmem = pl.BlockSpec(memory_space=pltpu.VMEM)
    return pl.pallas_call(
        pack_kernel,
        out_shape=[jax.ShapeDtypeStruct((32, cells + 128), BF16)] * 8,
        in_specs=[vmem, vmem, pl.BlockSpec(memory_space=pl.ANY)],
        out_specs=[vmem] * 8,
        scratch_shapes=[
            pltpu.VMEM((grains, cells), BF16),
            pltpu.VMEM((256, grains), BF16),
            pltpu.VMEM((16, grains), F32),
            pltpu.VMEM((128, grains), BF16),
            pltpu.SemaphoreType.DMA((4,)),
        ],
        name="pack",
    )(listed, poses, grids)


def spline(position):
    cells = lax.broadcasted_iota(jnp.int32, (GRID, position.shape[1]), 0).astype(F32)
    offset = position - cells
    distance = jnp.abs(offset)
    outer = 2.0 - distance
    inner = jnp.maximum(outer - distance, 0.0)
    outer = jnp.maximum(outer, 0.0)
    outer_sq = outer * outer
    inner_sq = inner * inner
    basis6 = outer_sq * outer - 0.5 * (inner_sq * inner)
    bend = inner_sq - outer_sq
    return basis6, jnp.where(offset < 0.0, -bend, bend)


def spread_rows(grid_rows, cell, values):
    for half in range(2):
        grid_rows[half, pl.ds(cell, values.shape[0], stride=GRID), :] = values[:, 128 * half:128 * half + 128]


def pair_partials(slot, pair, grid_rows, positions, product, partial):
    nodes = positions.shape[1] // 3
    cube_rows = pl.ds(pl.multiple_of(pair * GRID, GRID), GRID)
    cube = jnp.concatenate([grid_rows[half, cube_rows, :].astype(BF16) for half in range(2)], axis=1)
    spots = [positions[pl.ds(pair, 1), axis * nodes:axis * nodes + nodes] for axis in range(3)]
    basis_y, slope_y = spline(spots[1])
    basis_z, slope_z = spline(spots[2])
    for cell in range(GRID):
        plain = jnp.broadcast_to(basis_y[cell:cell + 1], basis_z.shape)
        tilt = jnp.broadcast_to(slope_y[cell:cell + 1], basis_z.shape)
        rows = slice(cell * GRID, cell * GRID + GRID)
        product[rows, 0:nodes] = (plain * basis_z).astype(BF16)
        product[rows, nodes:2 * nodes] = (tilt * basis_z).astype(BF16)
        product[rows, 2 * nodes:3 * nodes] = (plain * slope_z).astype(BF16)
    basis_x, slope_x = spline(spots[0])
    basis_x = (basis_x * (1.0 / 6.0)).astype(BF16).astype(F32)
    slope_x = (slope_x * 0.5).astype(BF16).astype(F32)
    sums = dot(cube, product[...])
    plain = sums[:, 0:nodes]
    for index, (weight, term) in enumerate(
        ((basis_x, plain), (slope_x, plain), (basis_x, sums[:, nodes:2 * nodes]), (basis_x, sums[:, 2 * nodes:]))
    ):
        both = weight * term
        both = both[0:8] + both[8:16]
        for half in range(2):
            partial[2 * index + half, slot * 8:slot * 8 + 8, :] = both[:, 128 * half:128 * half + 128]


def group_sums(partial, bodies):
    nodes = 2 * partial.shape[2]
    totals = []
    for index in range(4):
        halves = []
        for half in range(2):
            parts = [partial[2 * index + half, pl.ds(part, 8, stride=8), :] for part in range(8)]
            while len(parts) > 1:
                parts = [left + right for left, right in zip(parts[::2], parts[1::2])]
            halves.append(parts[0])
        totals.append(jnp.concatenate(halves, axis=1))
    push = jnp.maximum(-totals[0], 0.0)
    force = [push * totals[1], push * totals[2], push * totals[3]]
    lanes = lax.broadcasted_iota(jnp.int32, (8, 128), 1)
    result = jnp.zeros((8, 128), F32)
    for m in range(3):
        result = jnp.where(lanes == m, jnp.sum(force[m], axis=1, keepdims=True), result)
        for l in range(3):
            product = bodies[:, l * nodes:l * nodes + nodes] * force[m]
            result = jnp.where(lanes == 3 + 3 * l + m, jnp.sum(product, axis=1, keepdims=True), result)
    return result


def pair_loop(count, order, grid_rows, positions, bodies_of, results, product, partial, bodies):
    def group(index, carry):
        pairs = [order[index * 8 + slot] for slot in range(8)]
        for slot in range(8):
            bodies[slot:slot + 1, :] = bodies_of(pairs[slot])
            pair_partials(slot, pairs[slot], grid_rows, positions, product.at[slot % 2], partial)
        sums = group_sums(partial, bodies)
        for slot in range(8):
            results[pl.ds(pairs[slot], 1), :] = sums[slot:slot + 1]
        return carry

    lax.fori_loop(0, (count + 7) // 8, group, 0)


def own_kernel(first_s, sdf_s, live_s, first, sdf, listed, poses, grids, body_table, knots, offsets,
               results, positions, bodies_out, pose_pairs, targets, order_out,
               grid_rows, own_order, product, partial, bodies, padded, pieces):
    pairs, width = positions.shape
    grains = body_table.shape[0]
    signs = parity_signs()

    def sort_pair(pair, counts):
        own, ghost = counts
        live = live_s[pair]
        near = jnp.where(sdf_s[pair] < grains, 1, 0)
        own_order[own] = pair
        order_out[ghost] = pair
        return own + live * near, ghost + live * (1 - near)

    own, ghost = lax.fori_loop(0, pairs, sort_pair, (0, 0))
    own_last = own_order[jnp.maximum(own - 1, 0)]
    ghost_last = order_out[jnp.maximum(ghost - 1, 0)]
    for extra in range(8):
        own_order[own + extra] = own_last
        order_out[ghost + extra] = ghost_last
    order_out[143] = ghost

    results[...] = jnp.zeros_like(results)
    positions[...] = knots[...].astype(F32) + offsets[...]

    def copy_body(pair, carry):
        bodies_out[pl.ds(pair, 1), :] = body_table[pl.ds(first_s[pair], 1), :]
        return carry

    lax.fori_loop(0, pairs, copy_body, 0, unroll=8)

    rows = lax.broadcasted_iota(jnp.int32, (grains, pairs), 0)
    first_hot = jnp.where(rows == first[...], 1.0, 0.0).astype(BF16)
    sdf_hot32 = jnp.where(rows == sdf[...], 1.0, 0.0)
    pose_pieces(poses, pieces, padded)
    pose_pairs[0:48, :] = dot(pieces[...], first_hot)
    pose_pairs[48:96, :] = dot(pieces[...], sdf_hot32.astype(BF16))
    hot = sdf_hot32.T.astype(BF16)
    for cell in range(GRID):
        part = slice(cell * GRID * GRID, cell * GRID * GRID + GRID * GRID)
        spread_rows(grid_rows, cell, dot(hot, grids[:, part]))

    targets[...] = jnp.zeros_like(targets)
    for base, op in ((0, "A"), (128, "B"), (256, "C"), (288, "AC"), (320, "BC"), (384, "D"), (416, "BD"), (448, "AD")):
        targets[base:base + 32, :] = one_hot_rows(listed_column(listed, signs, op), grains)

    pair_loop(own, own_order, grid_rows, positions, lambda pair: bodies_out[pl.ds(pair, 1), :],
              results, product, partial, bodies)


def own_pairs(first, sdf, live, listed, poses, grids, body_table, knots, offsets):
    pairs, width = knots.shape
    grains, cells = grids.shape
    vmem = pl.BlockSpec(memory_space=pltpu.VMEM)
    smem = pl.BlockSpec(memory_space=pltpu.SMEM)
    return pl.pallas_call(
        own_kernel,
        out_shape=[
            jax.ShapeDtypeStruct((pairs, 128), F32),
            jax.ShapeDtypeStruct((pairs, width), F32),
            jax.ShapeDtypeStruct((pairs, width), F32),
            jax.ShapeDtypeStruct((96, pairs), F32),
            jax.ShapeDtypeStruct((512, grains), BF16),
            jax.ShapeDtypeStruct((144,), jnp.int32),
        ],
        in_specs=[smem] * 3 + [vmem] * 8,
        out_specs=[vmem] * 5 + [smem],
        scratch_shapes=[
            pltpu.VMEM((2, pairs * GRID, 128), F32),
            pltpu.SMEM((144,), jnp.int32),
            pltpu.VMEM((2, GRID * GRID, width), BF16),
            pltpu.VMEM((8, 64, 128), F32),
            pltpu.VMEM((8, width), F32),
            pltpu.VMEM((16, grains), F32),
            pltpu.VMEM((48, grains), BF16),
        ],
        cost_estimate=pl.CostEstimate(flops=6 * 10**9, bytes_accessed=16 * 10**6, transcendentals=0),
        name="own_pairs",
    )(first, sdf, live, first.reshape(1, pairs), sdf.reshape(1, pairs), listed, poses, grids, body_table, knots, offsets)


def joined(value, base):
    return value[base:base + 12] + value[base + 16:base + 28] + value[base + 32:base + 44]


def ghost_kernel(order, first, sdf, own_results, positions, bodies_in, pose_pairs, *refs):
    payloads = refs[:8]
    own_sum, load_a, load_b, load_c, load_d = refs[8:13]
    ghosts, results, grid_rows, product, partial, bodies = refs[13:]
    pairs = positions.shape[0]
    grains = own_sum.shape[1]
    cells = GRID * GRID * GRID
    signs = parity_signs()
    for index in range(8):
        ghosts[32 * index:32 * index + 32, :] = payloads[index][...]

    row = sdf[...]
    ghost = row - grains
    direction = jnp.right_shift(ghost, 5)
    slot = jnp.bitwise_and(ghost, 31)
    cell = direction + jnp.where(direction >= 4, 1, 0)
    third = jnp.where(cell >= 6, 2, jnp.where(cell >= 3, 1, 0))
    row_step = (third - 1) * signs[0]
    col_step = (cell - 3 * third - 1) * signs[1]
    buffer_row = jnp.zeros_like(row)
    place = jnp.zeros_like(row)
    bases = {"A": 0, "AC": 32, "AD": 64, "B": 128, "BD": 160, "BC": 192, "C": 256, "D": 384}
    for index, op in enumerate(OPS):
        row_want, col_want = steps_of(op)
        match = (row_step == row_want) & (col_step == col_want)
        buffer_row = jnp.where(match, 32 * index, buffer_row)
        place = jnp.where(match, bases[op], place)
    buffer_row = jnp.where(ghost >= 0, buffer_row + slot, -1)
    place = jnp.where(ghost >= 0, place + slot, -1)

    slot_rows = lax.broadcasted_iota(jnp.int32, (256, pairs), 0)
    slot_hot = jnp.where(slot_rows == buffer_row, 1.0, 0.0)
    hot = slot_hot.T.astype(BF16)
    for index in range(GRID):
        part = slice(index * GRID * GRID, index * GRID * GRID + GRID * GRID)
        spread_rows(grid_rows, index, dot(hot, ghosts[:, part]))
    ghost_pose = dot(ghosts[:, cells:].astype(F32).T.astype(BF16), slot_hot.astype(BF16))

    results[...] = own_results[...]
    pair_loop(order[143], order, grid_rows, positions, lambda pair: bodies_in[pl.ds(pair, 1), :],
              results, product, partial, bodies)

    sums = results[...].T
    pose_first = joined(pose_pairs[...], 0)
    pose_second = joined(pose_pairs[...], 48) + joined(ghost_pose, 0)
    take = lambda value, index: value[index:index + 1]
    total = [take(sums, m) * SCALES[m] for m in range(3)]
    moment = [[take(sums, 3 + 3 * l + m) * SCALES[m] for m in range(3)] for l in range(3)]
    turn_1 = [[take(pose_first, 3 + 3 * i + j) for j in range(3)] for i in range(3)]
    turn_2 = [[take(pose_second, 3 + 3 * i + j) for j in range(3)] for i in range(3)]
    apart = [take(pose_first, i) - take(pose_second, i) for i in range(3)]
    force = [turn_2[i][0] * total[0] + turn_2[i][1] * total[1] + turn_2[i][2] * total[2] for i in range(3)]
    half = [[turn_1[j][0] * moment[0][m] + turn_1[j][1] * moment[1][m] + turn_1[j][2] * moment[2][m]
             for m in range(3)] for j in range(3)]
    outer = [[half[j][0] * turn_2[k][0] + half[j][1] * turn_2[k][1] + half[j][2] * turn_2[k][2]
              for k in range(3)] for j in range(3)]
    first_moment = [outer[1][2] - outer[2][1], outer[2][0] - outer[0][2], outer[0][1] - outer[1][0]]
    crossed = [apart[1] * force[2] - apart[2] * force[1], apart[2] * force[0] - apart[0] * force[2],
               apart[0] * force[1] - apart[1] * force[0]]
    second_moment = [-(crossed[i] + first_moment[i]) for i in range(3)]
    zero = jnp.zeros_like(force[0])
    loads_1 = jnp.concatenate(force + first_moment + [zero, zero], axis=0)
    loads_2 = jnp.concatenate([-value for value in force] + second_moment + [zero, zero], axis=0)
    loads_1 = jnp.concatenate(split3_rows(loads_1), axis=0).astype(BF16)
    loads_2 = jnp.concatenate(split3_rows(loads_2), axis=0).astype(BF16)
    rows = lax.broadcasted_iota(jnp.int32, (grains, pairs), 0)
    first_hot = jnp.where(rows == first[...], 1.0, 0.0).astype(BF16)
    own_hot = jnp.where(rows == row, 1.0, 0.0).astype(BF16)
    place_hot = jnp.where(rows == place, 1.0, 0.0).astype(BF16)
    near = dot(loads_1, first_hot, NT) + dot(loads_2, own_hot, NT)
    own_sum[...] = near[0:8] + near[8:16] + near[16:24]
    far = dot(loads_2, place_hot, NT)
    far = far[0:8] + far[8:16] + far[16:24]
    for index, out in enumerate((load_a, load_b, load_c, load_d)):
        out[...] = far[:, 128 * index:128 * index + 128]


SCALES = (STIFFNESS / 1296.0, STIFFNESS / 432.0, STIFFNESS / 432.0)


def split3_rows(value):
    return [piece.astype(F32) for piece in split3(value)]


def ghost_pairs(order, first, sdf, own_results, positions, bodies, pose_pairs, payloads, grains):
    pairs, width = positions.shape
    vmem = pl.BlockSpec(memory_space=pltpu.VMEM)
    smem = pl.BlockSpec(memory_space=pltpu.SMEM)
    load = jax.ShapeDtypeStruct((8, 128), F32)
    return pl.pallas_call(
        ghost_kernel,
        out_shape=[jax.ShapeDtypeStruct((8, grains), F32)] + [load] * 4,
        in_specs=[smem] + [vmem] * 14,
        out_specs=[vmem] * 5,
        scratch_shapes=[
            pltpu.VMEM((256, payloads[0].shape[1]), BF16),
            pltpu.VMEM((pairs, 128), F32),
            pltpu.VMEM((2, pairs * GRID, 128), F32),
            pltpu.VMEM((2, GRID * GRID, width), BF16),
            pltpu.VMEM((8, 64, 128), F32),
            pltpu.VMEM((8, width), F32),
        ],
        name="ghost_pairs",
    )(order, first.reshape(1, pairs), sdf.reshape(1, pairs), own_results, positions, bodies, pose_pairs, *payloads)


def return_kernel(own_sum, load_a, load_b, load_c, load_d, targets, out):
    loads = jnp.concatenate([load_a[...], load_b[...], load_c[...], load_d[...]], axis=1)
    pieces = jnp.concatenate(split3_rows(loads), axis=0).astype(BF16)
    added = dot(pieces, targets[...])
    total = own_sum[...] + (added[0:8] + added[8:16] + added[16:24])
    out[...] = total[0:6]


def return_loads(own_sum, loads, targets):
    vmem = pl.BlockSpec(memory_space=pltpu.VMEM)
    return pl.pallas_call(
        return_kernel,
        out_shape=jax.ShapeDtypeStruct((6, own_sum.shape[1]), F32),
        in_specs=[vmem] * 6,
        out_specs=vmem,
        name="return_loads",
    )(own_sum, *loads, targets)


def swapped(block, op, rows, cols):
    route = []
    row_step, col_step = steps_of(op)
    for r in range(rows):
        for c in range(cols):
            to_r = r + row_step * (1 - 2 * (r % 2))
            to_c = c + col_step * (1 - 2 * (c % 2))
            if 0 <= to_r < rows and 0 <= to_c < cols:
                route.append((r * cols + c, to_r * cols + to_c))
    return lax.ppermute(block, ("row", "col"), route)


def local(rows, cols, sdf_grids, grain_poses, surface_nodes, send_list, pair_first, pair_sdf, pair_pose, pair_live,
          knot_cells, offsets):
    grains = sdf_grids.shape[0]
    listed = send_list.reshape(8, send_list.shape[3])
    swap = lambda block, op: swapped(block, op, rows, cols)
    packed = pack(listed, grain_poses, sdf_grids)
    payloads = [swap(block, op) for block, op in zip(packed, OPS)]
    results, positions, bodies, pose_pairs, targets, order = own_pairs(
        pair_first, pair_sdf, pair_live, listed, grain_poses, sdf_grids, surface_nodes, knot_cells, offsets)
    own_sum, load_a, load_b, load_c, load_d = ghost_pairs(
        order, pair_first, pair_sdf, results, positions, bodies, pose_pairs, payloads, grains)
    back_a, back_b = swap(load_a, "A"), swap(load_b, "B")
    lanes = lax.broadcasted_iota(jnp.int32, load_a.shape, 1)
    send_c = jnp.where(lanes < 32, load_c, jnp.where(lanes < 64, back_a, back_b))
    send_d = jnp.where(lanes < 32, load_d, jnp.where(lanes < 64, back_b, back_a))
    back_c, back_d = swap(send_c, "C"), swap(send_d, "D")
    return return_loads(own_sum, (back_a, back_b, back_c, back_d), targets)


def solution(mesh):
    in_specs = (
        P(("row", "col"), None),
        P(None, ("row", "col")),
        P(("row", "col"), None),
        P("row", "col", None, None),
        P(("row", "col")),
        P(("row", "col")),
        P(("row", "col")),
        P(("row", "col")),
        P(("row", "col"), None),
        P(("row", "col"), None),
    )
    out_specs = P(None, ("row", "col"))
    body = functools.partial(local, mesh.shape["row"], mesh.shape["col"])
    return jax.shard_map(body, mesh=mesh, in_specs=in_specs, out_specs=out_specs, check_vma=False)
```

time: 169 us -> 72.3 us (0.43)
  the two profiles are of different devices: /device:TPU:25 before, /device:TPU:98 now
where the time goes in v1:
time: 72.3 us; the launch traced here: 72.2 us
  starting transfers between devices  33.4 us (46%)
  Pallas kernels  25.4 us (35%)
  waiting for transfers between devices  10.8 us (15%)
  local copies, waits for them, and re-layouts  1.57 us (2%)
    ppermute x12, starting transfers between devices, swapped(): return lax.ppermute(block, ('row', 'col'), route)  33.4 us
    ppermute x12, waiting for transfers between devices, swapped(): return lax.ppermute(block, ('row', 'col'), route)  10.8 us
    pallas_call x1, Pallas kernels, own_pairs(): pl.pallas_call(own_kernel, out_shape=[jax.ShapeDtypeStruct((pairs, 128),...  10.4 us
    pallas_call x1, Pallas kernels, ghost_pairs(): pl.pallas_call(ghost_kernel, out_shape=[jax.ShapeDtypeStruct((8, grains),...  8.1 us
    pallas_call x1, Pallas kernels, pack(): pl.pallas_call(pack_kernel, out_shape=[jax.ShapeDtypeStruct((32, cells +...  5.09 us
    pallas_call x1, Pallas kernels, return_loads(): pl.pallas_call(return_kernel, out_shape=jax.ShapeDtypeStruct((6, own_sum....  1.88 us
    unnamed x24, local copies, waits for them, and re-layouts  1.57 us
  transfers between devices with their start and end apart: 12, of which 3 were waited for; matrix products, arithmetic and copies ran while one was open for 0% of the time, Pallas kernels for 14%

profile of v1, /device:TPU:98, one launch (start us, length us, event | category | flops | bytes accessed | tf_op | source)
XLA Modules:
  0.0 72.2 jit_solution(12745106853214186540)
XLA Ops:
  0.0 5.1 %pack.1 = (bf16[32,4224]{1,0:T(8,128)(2,1)}, bf16[32,4224]{1,0:T(8,128)(2,1)}, bf16[32,4224]{1,0:T(8,128)(2,1)}, bf16[32,4224]{1,0:T(8,128)(2,1)}, bf16[32,4224]...) custom-call(s32[8,32]{1,0:T(8,128)} %bitcast.3, ...), custom_call_target="tpu_custom_call" | custom-call | tf_op jit(solution)/shard_map/pack/pallas_call | solution.py:98
  5.1 1.7 %collective-permute-start = (bf16[32,4224]{1,0:T(8,128)(2,1)}, bf16[32,4224]{1,0:T(8,128)(2,1)S(1)}, u32[]{:S(2)}, u32[]{:S(2)}) collective-permute-start(bf16[32,4224]{1,0:T(8,128)(2,1)} %get-tuple-element.29), channel_id=1, source_target_pairs={{0,1},{1,0},{2,3},{3,2},{4,5},{5,4},{6,7},{7,6},{8,9},{9,8},{10,11... | collective-permute-start | bytes 811016 | tf_op jit(solution)/shard_map/ppermute | solution.py:418
  6.8 3.9 %collective-permute-start.1 = (bf16[32,4224]{1,0:T(8,128)(2,1)}, bf16[32,4224]{1,0:T(8,128)(2,1)S(1)}, u32[]{:S(2)}, u32[]{:S(2)}) collective-permute-start(bf16[32,4224]{1,0:T(8,128)(2,1)} %get-tuple-element.30), channel_id=1, source_target_pairs={{1,2},{2,1},{3,4},{4,3},{5,6},{6,5},{7,8},{8,7},{9,10},{10,9},{11,... | collective-permute-start | bytes 811016 | tf_op jit(solution)/shard_map/ppermute | solution.py:418
  10.7 0.1 collective-permute-start.2
  10.8 2.9 %collective-permute-start.3 = (bf16[32,4224]{1,0:T(8,128)(2,1)}, bf16[32,4224]{1,0:T(8,128)(2,1)S(1)}, u32[]{:S(2)}, u32[]{:S(2)}) collective-permute-start(bf16[32,4224]{1,0:T(8,128)(2,1)} %get-tuple-element.32), channel_id=1, source_target_pairs={{1,18},{2,17},{3,20},{4,19},{5,22},{6,21},{7,24},{8,23},{9,26},{10... | collective-permute-start | bytes 811016 | tf_op jit(solution)/shard_map/ppermute | solution.py:418
  13.7 2.6 %collective-permute-start.4 = (bf16[32,4224]{1,0:T(8,128)(2,1)}, bf16[32,4224]{1,0:T(8,128)(2,1)S(1)}, u32[]{:S(2)}, u32[]{:S(2)}) collective-permute-start(bf16[32,4224]{1,0:T(8,128)(2,1)} %get-tuple-element.33), channel_id=1, source_target_pairs={{16,33},{17,32},{18,35},{19,34},{20,37},{21,36},{22,39},{23,38},{2... | collective-permute-start | bytes 811016 | tf_op jit(solution)/shard_map/ppermute | solution.py:418
  16.3 0.0 collective-permute-done.refs_0_
  16.3 4.7 %collective-permute-start.5 = (bf16[32,4224]{1,0:T(8,128)(2,1)}, bf16[32,4224]{1,0:T(8,128)(2,1)S(1)}, u32[]{:S(2)}, u32[]{:S(2)}) collective-permute-start(bf16[32,4224]{1,0:T(8,128)(2,1)} %get-tuple-element.34), channel_id=1, source_target_pairs={{17,34},{18,33},{19,36},{20,35},{21,38},{22,37},{23,40},{24,39},{2... | collective-permute-start | bytes 811016 | tf_op jit(solution)/shard_map/ppermute | solution.py:418
  21.1 0.0 collective-permute-done.1.refs_1_
  21.1 1.3 %collective-permute-start.6 = (bf16[32,4224]{1,0:T(8,128)(2,1)}, bf16[32,4224]{1,0:T(8,128)(2,1)S(1)}, u32[]{:S(2)}, u32[]{:S(2)}) collective-permute-start(bf16[32,4224]{1,0:T(8,128)(2,1)} %get-tuple-element.35), channel_id=1, source_target_pairs={{0,16},{1,17},{2,18},{3,19},{4,20},{5,21},{6,22},{7,23},{8,24},{9,... | collective-permute-start | bytes 811016 | tf_op jit(solution)/shard_map/ppermute | solution.py:418
  22.4 2.0 %collective-permute-done.2.refs_2_ = bf16[32,4224]{1,0:T(8,128)(2,1)S(1)} collective-permute-done((bf16[32,4224]{1,0:T(8,128)(2,1)}, bf16[32,4224]{1,0:T(8,128)(2,1)S(1)}, u32[]{:S(2)}, u32[]{:S(2)}) %collective-permute-start.2) | collective-permute-done | bytes 270368 | tf_op jit(solution)/shard_map/ppermute | solution.py:418
  24.4 1.9 %collective-permute-start.7 = (bf16[32,4224]{1,0:T(8,128)(2,1)}, bf16[32,4224]{1,0:T(8,128)(2,1)S(1)}, u32[]{:S(2)}, u32[]{:S(2)}) collective-permute-start(bf16[32,4224]{1,0:T(8,128)(2,1)} %get-tuple-element.36), channel_id=1, source_target_pairs={{16,32},{17,33},{18,34},{19,35},{20,36},{21,37},{22,38},{23,39},{2... | collective-permute-start | bytes 811016 | tf_op jit(solution)/shard_map/ppermute | solution.py:418
  26.3 10.4 %own_pairs.1 = (f32[128,128]{1,0:T(8,128)}, f32[128,768]{1,0:T(8,128)}, f32[128,768]{1,0:T(8,128)}, f32[96,128]{1,0:T(8,128)}, bf16[512,512]{1,0:T(8,128)(2,1)}, /*index=5*/s32[144]{0:T(256)}) custom-call(s32[128]{0:T(128)} %first_s.1, s32[128]{0:T(128)} %sdf_s.1, s32[128]{0:T(128)} %live_s.1, s32[1,128]{1,0:T(1,128)} %bitcast.5, s32[1,128]{1,0:T(1,128)} %bitcast.7, ...), custom_call_target="tpu_custom_call" | custom-call | flops 6000000000 | bytes 16000000 | tf_op jit(solution)/shard_map/own_pairs/pallas_call | solution.py:254
  36.7 0.0 collective-permute-done.3.refs_3_
  36.7 0.0 collective-permute-done.4.refs_4_
  36.8 0.0 collective-permute-done.5.refs_5_
  36.8 0.0 collective-permute-done.7.refs_7_
  36.8 0.6 copy-done.3
  37.5 0.1 copy-done.4
  37.5 0.1 copy-done.5
  37.6 0.1 copy-done.6
  37.7 0.1 copy-done.7
  37.8 8.1 %ghost_pairs.1 = (f32[8,512]{1,0:T(8,128)}, f32[8,128]{1,0:T(8,128)}, f32[8,128]{1,0:T(8,128)}, f32[8,128]{1,0:T(8,128)}, f32[8,128]{1,0:T(8,128)}) custom-call(s32[144]{0:T(256)} %get-tuple-element.24.order, s32[1,128]{1,0:T(1,128)} %bitcast.6, s32[1,128]{1,0:T(1,128)} %bitcast.8, f32[128,128]{1,0:T(8,128)} %get-tuple-element.25.own_results, ...), custom_call_target="tpu_custom_call" | custom-call | tf_op jit(solution)/shard_map/ghost_pairs/pallas_call | solution.py:373
  45.9 8.4 %collective-permute-start.8 = (f32[8,128]{1,0:T(8,128)}, f32[8,128]{1,0:T(8,128)S(1)}, u32[]{:S(2)}, u32[]{:S(2)}) collective-permute-start(f32[8,128]{1,0:T(8,128)} %get-tuple-element.38), channel_id=1, source_target_pairs={{0,16},{1,17},{2,18},{3,19},{4,20},{5,21},{6,22},{7,23},{8,24},{9,... | collective-permute-start | bytes 12296 | tf_op jit(solution)/shard_map/ppermute | solution.py:418
  54.3 1.9 %collective-permute-start.9 = (f32[8,128]{1,0:T(8,128)}, f32[8,128]{1,0:T(8,128)S(1)}, u32[]{:S(2)}, u32[]{:S(2)}) collective-permute-start(f32[8,128]{1,0:T(8,128)} %get-tuple-element.39), channel_id=1, source_target_pairs={{16,32},{17,33},{18,34},{19,35},{20,36},{21,37},{22,38},{23,39},{2... | collective-permute-start | bytes 12296 | tf_op jit(solution)/shard_map/ppermute | solution.py:418
  56.3 3.2 %collective-permute-done.9.load_b = f32[8,128]{1,0:T(8,128)S(1)} collective-permute-done((f32[8,128]{1,0:T(8,128)}, f32[8,128]{1,0:T(8,128)S(1)}, u32[]{:S(2)}, u32[]{:S(2)}) %collective-permute-start.9) | collective-permute-done | bytes 4128 | tf_op jit(solution)/shard_map/ppermute | solution.py:418
  59.4 0.7 select_select_fusion
  60.1 2.0 %collective-permute-start.10 = (f32[8,128]{1,0:T(8,128)S(1)}, f32[8,128]{1,0:T(8,128)S(1)}, u32[]{:S(2)}, u32[]{:S(2)}) collective-permute-start(f32[8,128]{1,0:T(8,128)S(1)} %get-tuple-element.44), channel_id=1, source_target_pairs={{0,1},{1,0},{2,3},{3,2},{4,5},{5,4},{6,7},{7,6},{8,9},{9,8},{10,11... | collective-permute-start | bytes 12296 | tf_op jit(solution)/shard_map/ppermute | solution.py:418
  62.1 2.0 %collective-permute-start.11 = (f32[8,128]{1,0:T(8,128)S(1)}, f32[8,128]{1,0:T(8,128)S(1)}, u32[]{:S(2)}, u32[]{:S(2)}) collective-permute-start(f32[8,128]{1,0:T(8,128)S(1)} %get-tuple-element.43), channel_id=1, source_target_pairs={{1,2},{2,1},{3,4},{4,3},{5,6},{6,5},{7,8},{8,7},{9,10},{10,9},{11,... | collective-permute-start | bytes 12296 | tf_op jit(solution)/shard_map/ppermute | solution.py:418
  64.1 5.6 %collective-permute-done.11.load_d = f32[8,128]{1,0:T(8,128)S(1)} collective-permute-done((f32[8,128]{1,0:T(8,128)S(1)}, f32[8,128]{1,0:T(8,128)S(1)}, u32[]{:S(2)}, u32[]{:S(2)}) %collective-permute-start.11) | collective-permute-done | bytes 4128 | tf_op jit(solution)/shard_map/ppermute | solution.py:418
  69.8 0.6 copy-done.11
  70.3 1.9 %return_loads.1 = f32[6,512]{1,0:T(8,128)} custom-call(f32[8,512]{1,0:T(8,128)} %get-tuple-element.37.own_sum, f32[8,128]{1,0:T(8,128)} %copy-done.8, f32[8,128]{1,0:T(8,128)} %copy-done.9, f32[8,128]{1,0:T(8,128)} %copy-done.10, f32[8,128]{1,0:T(8,128)} %copy-done.11, bf16[512,512]{1,0:T(8,128)(2,1)} %get-tuple-element.42.targets), custom_call_target="tpu_custom_call" | custom-call | tf_op jit(solution)/shard_map/return_loads/pallas_call | solution.py:400
  (22 shorter events, 0.0 us)
Async XLA Ops:
  5.1 11.2 %collective-permute-start = (bf16[32,4224]{1,0:T(8,128)(2,1)}, bf16[32,4224]{1,0:T(8,128)(2,1)S(1)}, u32[]{:S(2)}, u32[]{:S(2)}) collective-permute-start(bf16[32,4224]{1,0:T(8,128)(2,1)} %get-tuple-element.29), channel_id=1, source_target_pairs={{0,1},{1,0},{2,3},{3,2},{4,5},{5,4},{6,7},{7,6},{8,9},{9,8},{10,11... | collective-permute-start | bytes 811016 | tf_op jit(solution)/shard_map/ppermute | solution.py:418
  6.8 14.3 %collective-permute-start.1 = (bf16[32,4224]{1,0:T(8,128)(2,1)}, bf16[32,4224]{1,0:T(8,128)(2,1)S(1)}, u32[]{:S(2)}, u32[]{:S(2)}) collective-permute-start(bf16[32,4224]{1,0:T(8,128)(2,1)} %get-tuple-element.30), channel_id=1, source_target_pairs={{1,2},{2,1},{3,4},{4,3},{5,6},{6,5},{7,8},{8,7},{9,10},{10,9},{11,... | collective-permute-start | bytes 811016 | tf_op jit(solution)/shard_map/ppermute | solution.py:418
  10.7 13.7 %collective-permute-start.2 = (bf16[32,4224]{1,0:T(8,128)(2,1)}, bf16[32,4224]{1,0:T(8,128)(2,1)S(1)}, u32[]{:S(2)}, u32[]{:S(2)}) collective-permute-start(bf16[32,4224]{1,0:T(8,128)(2,1)} %get-tuple-element.31), channel_id=1, source_target_pairs={{0,17},{1,16},{2,19},{3,18},{4,21},{5,20},{6,23},{7,22},{8,25},{9,... | collective-permute-start | bytes 811016 | tf_op jit(solution)/shard_map/ppermute | solution.py:418
  10.8 26.0 %collective-permute-start.3 = (bf16[32,4224]{1,0:T(8,128)(2,1)}, bf16[32,4224]{1,0:T(8,128)(2,1)S(1)}, u32[]{:S(2)}, u32[]{:S(2)}) collective-permute-start(bf16[32,4224]{1,0:T(8,128)(2,1)} %get-tuple-element.32), channel_id=1, source_target_pairs={{1,18},{2,17},{3,20},{4,19},{5,22},{6,21},{7,24},{8,23},{9,26},{10... | collective-permute-start | bytes 811016 | tf_op jit(solution)/shard_map/ppermute | solution.py:418
  13.7 23.1 %collective-permute-start.4 = (bf16[32,4224]{1,0:T(8,128)(2,1)}, bf16[32,4224]{1,0:T(8,128)(2,1)S(1)}, u32[]{:S(2)}, u32[]{:S(2)}) collective-permute-start(bf16[32,4224]{1,0:T(8,128)(2,1)} %get-tuple-element.33), channel_id=1, source_target_pairs={{16,33},{17,32},{18,35},{19,34},{20,37},{21,36},{22,39},{23,38},{2... | collective-permute-start | bytes 811016 | tf_op jit(solution)/shard_map/ppermute | solution.py:418
  16.3 20.4 %copy-start = (bf16[32,4224]{1,0:T(8,128)(2,1)}, bf16[32,4224]{1,0:T(8,128)(2,1)S(1)}, u32[]{:S(2)}) copy-start(bf16[32,4224]{1,0:T(8,128)(2,1)S(1)} %collective-permute-done.refs_0_) | copy-start | bytes 811012
  16.3 20.4 %collective-permute-start.5 = (bf16[32,4224]{1,0:T(8,128)(2,1)}, bf16[32,4224]{1,0:T(8,128)(2,1)S(1)}, u32[]{:S(2)}, u32[]{:S(2)}) collective-permute-start(bf16[32,4224]{1,0:T(8,128)(2,1)} %get-tuple-element.34), channel_id=1, source_target_pairs={{17,34},{18,33},{19,36},{20,35},{21,38},{22,37},{23,40},{24,39},{2... | collective-permute-start | bytes 811016 | tf_op jit(solution)/shard_map/ppermute | solution.py:418
  21.1 15.6 %copy-start.1 = (bf16[32,4224]{1,0:T(8,128)(2,1)}, bf16[32,4224]{1,0:T(8,128)(2,1)S(1)}, u32[]{:S(2)}) copy-start(bf16[32,4224]{1,0:T(8,128)(2,1)S(1)} %collective-permute-done.1.refs_1_) | copy-start | bytes 811012
  21.1 15.7 %collective-permute-start.6 = (bf16[32,4224]{1,0:T(8,128)(2,1)}, bf16[32,4224]{1,0:T(8,128)(2,1)S(1)}, u32[]{:S(2)}, u32[]{:S(2)}) collective-permute-start(bf16[32,4224]{1,0:T(8,128)(2,1)} %get-tuple-element.35), channel_id=1, source_target_pairs={{0,16},{1,17},{2,18},{3,19},{4,20},{5,21},{6,22},{7,23},{8,24},{9,... | collective-permute-start | bytes 811016 | tf_op jit(solution)/shard_map/ppermute | solution.py:418
  24.4 12.3 %copy-start.2 = (bf16[32,4224]{1,0:T(8,128)(2,1)}, bf16[32,4224]{1,0:T(8,128)(2,1)S(1)}, u32[]{:S(2)}) copy-start(bf16[32,4224]{1,0:T(8,128)(2,1)S(1)} %collective-permute-done.2.refs_2_) | copy-start | bytes 811012
  24.4 12.4 %collective-permute-start.7 = (bf16[32,4224]{1,0:T(8,128)(2,1)}, bf16[32,4224]{1,0:T(8,128)(2,1)S(1)}, u32[]{:S(2)}, u32[]{:S(2)}) collective-permute-start(bf16[32,4224]{1,0:T(8,128)(2,1)} %get-tuple-element.36), channel_id=1, source_target_pairs={{16,32},{17,33},{18,34},{19,35},{20,36},{21,37},{22,38},{23,39},{2... | collective-permute-start | bytes 811016 | tf_op jit(solution)/shard_map/ppermute | solution.py:418
  36.7 0.7 %copy-start.3 = (bf16[32,4224]{1,0:T(8,128)(2,1)}, bf16[32,4224]{1,0:T(8,128)(2,1)S(1)}, u32[]{:S(2)}) copy-start(bf16[32,4224]{1,0:T(8,128)(2,1)S(1)} %collective-permute-done.3.refs_3_) | copy-start | bytes 811012
  36.8 0.8 %copy-start.4 = (bf16[32,4224]{1,0:T(8,128)(2,1)}, bf16[32,4224]{1,0:T(8,128)(2,1)S(1)}, u32[]{:S(2)}) copy-start(bf16[32,4224]{1,0:T(8,128)(2,1)S(1)} %collective-permute-done.4.refs_4_) | copy-start | bytes 811012
  36.8 0.8 %copy-start.5 = (bf16[32,4224]{1,0:T(8,128)(2,1)}, bf16[32,4224]{1,0:T(8,128)(2,1)S(1)}, u32[]{:S(2)}) copy-start(bf16[32,4224]{1,0:T(8,128)(2,1)S(1)} %collective-permute-done.5.refs_5_) | copy-start | bytes 811012
  36.8 0.9 %copy-start.6 = (bf16[32,4224]{1,0:T(8,128)(2,1)}, bf16[32,4224]{1,0:T(8,128)(2,1)S(1)}, u32[]{:S(2)}) copy-start(bf16[32,4224]{1,0:T(8,128)(2,1)S(1)} %collective-permute-done.6.refs_6_) | copy-start | bytes 811012
  36.8 1.0 %copy-start.7 = (bf16[32,4224]{1,0:T(8,128)(2,1)}, bf16[32,4224]{1,0:T(8,128)(2,1)S(1)}, u32[]{:S(2)}) copy-start(bf16[32,4224]{1,0:T(8,128)(2,1)S(1)} %collective-permute-done.7.refs_7_) | copy-start | bytes 811012
  45.9 10.4 %collective-permute-start.8 = (f32[8,128]{1,0:T(8,128)}, f32[8,128]{1,0:T(8,128)S(1)}, u32[]{:S(2)}, u32[]{:S(2)}) collective-permute-start(f32[8,128]{1,0:T(8,128)} %get-tuple-element.38), channel_id=1, source_target_pairs={{0,16},{1,17},{2,18},{3,19},{4,20},{5,21},{6,22},{7,23},{8,24},{9,... | collective-permute-start | bytes 12296 | tf_op jit(solution)/shard_map/ppermute | solution.py:418
  54.3 5.1 %collective-permute-start.9 = (f32[8,128]{1,0:T(8,128)}, f32[8,128]{1,0:T(8,128)S(1)}, u32[]{:S(2)}, u32[]{:S(2)}) collective-permute-start(f32[8,128]{1,0:T(8,128)} %get-tuple-element.39), channel_id=1, source_target_pairs={{16,32},{17,33},{18,34},{19,35},{20,36},{21,37},{22,38},{23,39},{2... | collective-permute-start | bytes 12296 | tf_op jit(solution)/shard_map/ppermute | solution.py:418
  56.3 13.5 %copy-start.8 = (f32[8,128]{1,0:T(8,128)}, f32[8,128]{1,0:T(8,128)S(1)}, u32[]{:S(2)}) copy-start(f32[8,128]{1,0:T(8,128)S(1)} %collective-permute-done.8.load_a) | copy-start | bytes 12292
  59.4 10.3 %copy-start.9 = (f32[8,128]{1,0:T(8,128)}, f32[8,128]{1,0:T(8,128)S(1)}, u32[]{:S(2)}) copy-start(f32[8,128]{1,0:T(8,128)S(1)} %collective-permute-done.9.load_b) | copy-start | bytes 12292
  60.1 4.0 %collective-permute-start.10 = (f32[8,128]{1,0:T(8,128)S(1)}, f32[8,128]{1,0:T(8,128)S(1)}, u32[]{:S(2)}, u32[]{:S(2)}) collective-permute-start(f32[8,128]{1,0:T(8,128)S(1)} %get-tuple-element.44), channel_id=1, source_target_pairs={{0,1},{1,0},{2,3},{3,2},{4,5},{5,4},{6,7},{7,6},{8,9},{9,8},{10,11... | collective-permute-start | bytes 12296 | tf_op jit(solution)/shard_map/ppermute | solution.py:418
  62.1 7.6 %collective-permute-start.11 = (f32[8,128]{1,0:T(8,128)S(1)}, f32[8,128]{1,0:T(8,128)S(1)}, u32[]{:S(2)}, u32[]{:S(2)}) collective-permute-start(f32[8,128]{1,0:T(8,128)S(1)} %get-tuple-element.43), channel_id=1, source_target_pairs={{1,2},{2,1},{3,4},{4,3},{5,6},{6,5},{7,8},{8,7},{9,10},{10,9},{11,... | collective-permute-start | bytes 12296 | tf_op jit(solution)/shard_map/ppermute | solution.py:418
  64.1 5.6 %copy-start.10 = (f32[8,128]{1,0:T(8,128)}, f32[8,128]{1,0:T(8,128)S(1)}, u32[]{:S(2)}) copy-start(f32[8,128]{1,0:T(8,128)S(1)} %collective-permute-done.10.load_c) | copy-start | bytes 12292
  69.7 0.6 copy-start.11
